TPU v7x, 512 devices: a whole 4x8x8 slice. The times are simulated.
512 devices in a mesh: grp: 8 (over z_hi, core), shard: 64 (over z_lo, y, x).
Axes of the slice: x: 4, y: 8, z: 8 (z_hi: 4, z_lo: 2; z = z_hi * 2 + z_lo), core: 2. Of those that a mesh axis runs over, the one named last changes fastest.
Arguments:
- gradients: float32 [8, 1024, 512], P('grp', 'shard'), may hold values from -6 to 6
- weight: float32 [1024, 512], P('shard'), may hold values from -0.1875 to 0.1875
- moment: float32 [1024, 512], P('shard'), may hold values from -4 to 4
- second: float32 [1024, 512], P('shard'), may hold values from 0.01 to 0.5
- left_gram: float32 [1024, 1024], P('shard'), may hold values from -3 to 60, as said below
- left_basis: float32 [1024, 1024], P('shard'), may hold values from -0.1 to 1.1, as said below
- right_gram: float32 [512, 512], P('shard'), may hold values from -3 to 60, as said below
- right_basis: float32 [512, 512], P('shard'), may hold values from -0.1 to 1.1, as said below
Outputs:
- weight_new: float32 [1024, 512], P('shard')
- moment_new: float32 [1024, 512], P('shard')
- second_new: float32 [1024, 512], P('shard')
- left_new: float32 [1024, 1024], P('shard')
- left_basis_new: float32 [1024, 1024], P('shard')
- right_new: float32 [512, 512], P('shard')
- right_basis_new: float32 [512, 512], P('shard')
Inputs may be any that keep to these rules, and one draw needn't show every extreme that they name: `left_gram`: symmetric positive definite. `right_gram`: symmetric positive definite. `left_basis`: square and of full rank. `right_basis`: square and of full rank.
All inputs are finite; a program needn't handle non-finite values.
Results may differ from a plain program's by a relative error of at most 0.0015.
The roundings to bfloat16 on the way count: a program that leaves them out, or rounds other values in their place, can miss the bound.
Values may be sent and summed in bfloat16 or wider, within the bound.
No kernel may reach another device: no remote copies, remote signals or barrier semaphores. Data moves between devices by JAX's collectives and lax.ppermute only.
A program may use at most 64 MiB of HBM per device.

v0:
```python
import jax
import jax.numpy as jnp
from jax import lax
from jax.sharding import PartitionSpec as P

NS_ITERS = 2
BETA_ONE = 0.9
BETA_TWO = 0.95
GRAM_DECAY = 0.95
ADAM_EPS = 1e-08
NORM_EPS = 1e-06
STEP_SIZE = 0.02
START_SCALE = 0.75
PRECISE = lax.Precision.HIGHEST


def inner_rows(former, latter):
    return lax.dot_general(
        former, latter, (((0,), (0,)), ((), ())), preferred_element_type=jnp.float32
    )


def outer_rows(former, latter):
    return lax.dot_general(
        former, latter, (((1,), (1,)), ((), ())), preferred_element_type=jnp.float32
    )


def start_rows(power_rows, column_sums):
    scaled = START_SCALE * power_rows / jnp.sqrt(column_sums + NORM_EPS)
    return lax.optimization_barrier(scaled.astype(jnp.bfloat16))


def left_sweep(current):
    segment = lax.all_gather(current, "shard", axis=0, tiled=True)
    square = outer_rows(current, segment).astype(jnp.bfloat16)
    running = jnp.dot(square, segment, preferred_element_type=jnp.float32)
    return 1.5 * current.astype(jnp.float32) - 0.5 * running


def right_sweep(current):
    segment = lax.all_gather(current, "shard", axis=0, tiled=True)
    square = outer_rows(current, segment).astype(jnp.bfloat16)
    running = jnp.dot(square, segment, preferred_element_type=jnp.float32)
    return 1.5 * current.astype(jnp.float32) - 0.5 * running


def local(gradients, weight, moment, second, left_gram, left_basis, right_gram, right_basis):
    local_rows = weight.shape[0]
    right_rows = right_gram.shape[0]
    row_first = lax.axis_index("shard") * local_rows
    right_first = lax.axis_index("shard") * right_rows
    gradient = lax.psum(gradients[0], "grp") / lax.axis_size("grp")
    moment_new = BETA_ONE * moment + (1.0 - BETA_ONE) * gradient
    grad_half = gradient.astype(jnp.bfloat16)
    moment_half = moment_new.astype(jnp.bfloat16)
    left_half = left_basis.astype(jnp.bfloat16)
    right_whole = lax.all_gather(right_basis.astype(jnp.bfloat16), "shard", axis=0, tiled=True)
    right_wide = lax.optimization_barrier(right_whole).astype(jnp.float32)
    basis_part = lax.all_gather(left_half, "shard", axis=0, tiled=True)
    grad_part = lax.all_gather(grad_half, "shard", axis=0, tiled=True)
    basis_columns = lax.dynamic_slice_in_dim(basis_part, row_first, local_rows, 1)
    turned = inner_rows(basis_columns, grad_part)
    gram_block = GRAM_DECAY * left_gram + (1.0 - GRAM_DECAY) * outer_rows(grad_half, grad_part)
    power_rows = jnp.dot(gram_block, basis_part.astype(jnp.float32), precision=PRECISE)
    grad_columns = lax.dynamic_slice_in_dim(grad_part, right_first, right_rows, 1)
    right_terms = inner_rows(grad_columns, grad_part)
    core_state, basis_columns = ((turned, gram_block, power_rows, right_terms), basis_columns)
    core_state, turned_moment = (
        core_state,
        inner_rows(basis_columns, lax.all_gather(moment_half, "shard", axis=0, tiled=True)),
    )
    turned_grad, left_new, left_power, right_terms = core_state
    right_new = GRAM_DECAY * right_gram + (1.0 - GRAM_DECAY) * right_terms
    rotated_grad = jnp.dot(
        turned_grad.astype(jnp.bfloat16), right_whole, preferred_element_type=jnp.float32
    )
    rotated_moment = jnp.dot(
        turned_moment.astype(jnp.bfloat16), right_whole, preferred_element_type=jnp.float32
    )
    second_new = BETA_TWO * second + (1.0 - BETA_TWO) * rotated_grad * rotated_grad
    direction = (rotated_moment / (jnp.sqrt(second_new) + ADAM_EPS)).astype(jnp.bfloat16)
    returned = outer_rows(direction, right_whole).astype(jnp.bfloat16)
    update = jnp.dot(
        left_half,
        lax.all_gather(returned, "shard", axis=0, tiled=True),
        preferred_element_type=jnp.float32,
    )
    weight_new = weight - STEP_SIZE * update
    right_power = jnp.dot(right_new, right_wide, precision=PRECISE)
    left_sums, right_sums = lax.psum(
        (jnp.sum(left_power * left_power, axis=0), jnp.sum(right_power * right_power, axis=0)),
        "shard",
    )
    right_current = start_rows(right_power, right_sums)
    right_result = right_power
    for sweep in range(NS_ITERS):
        right_result = right_sweep(right_current)
        right_current = lax.optimization_barrier(right_result.astype(jnp.bfloat16))
    left_current = start_rows(left_power, left_sums)
    left_result = left_power
    for sweep in range(NS_ITERS):
        left_result = left_sweep(left_current)
        left_current = lax.optimization_barrier(left_result.astype(jnp.bfloat16))
    return (weight_new, moment_new, second_new, left_new, left_result, right_new, right_result)


def solution(mesh):
    return jax.shard_map(
        local,
        mesh=mesh,
        in_specs=(
            P("grp", "shard", None),
            P("shard", None),
            P("shard", None),
            P("shard", None),
            P("shard", None),
            P("shard", None),
            P("shard", None),
            P("shard", None),
        ),
        out_specs=(
            P("shard", None),
            P("shard", None),
            P("shard", None),
            P("shard", None),
            P("shard", None),
            P("shard", None),
            P("shard", None),
        ),
        check_vma=False,
    )
```

profile of v0, /device:TPU:2, one launch (start us, length us, event | category | flops | bytes accessed | tf_op | source)
XLA Modules:
  0.0 1857.0 jit_solution(10023106520451230898)
XLA Ops:
  7.2 0.0 copy-start.8
  7.2 0.0 all-gather.11.cloned.1.call-start
  7.2 36.2 %psum.21 = f32[16,512]{1,0:T(8,128)S(1)} all-reduce(f32[16,512]{1,0:T(8,128)} %bitcast.32), channel_id=1, replica_groups=mesh['grp'=8,'shard'=64] {'grp'}, use_global_device_ids=true, to_apply=%region_0.0 | all-reduce | flops 8192 | bytes 65536 | tf_op jit(solution)/shard_map/psum | solution.py:53
  43.4 1.4 fusion.29
  44.8 0.0 copy-start.5
  44.8 0.0 all-gather.11.cloned.1.call-update
  44.8 0.0 all-gather.7.cloned.1.call-start
  44.9 1.5 convert_element_type.62
  46.3 0.0 all-gather.7.cloned.1.call-update
  46.4 0.0 all-gather.9.cloned.1.call-start
  46.4 0.7 all-gather.9.cloned.1.call-update
  47.1 0.0 all-gather.15.cloned.1.call-start
  47.1 0.7 convert_element_type.65
  47.9 154.5 %all_gather.29 = bf16[512,512]{1,0:T(8,128)(2,1)S(1)} all-gather(bf16[8,512]{1,0:T(8,128)(2,1)S(1)} %convert_element_type.65), channel_id=1, replica_groups=mesh['grp'=8,'shard'=64] {'shard'}, dimensions={0}, use_global_device_ids=true | all-gather | bytes 532480 | tf_op jit(solution)/shard_map/all_gather | solution.py:58
  202.3 138.1 %all-gather.11.cloned.1.call-done = bf16[1024,512]{1,0:T(8,128)(2,1)} async-done(((bf16[16,512]{1,0:T(8,128)(2,1)}), bf16[1024,512]{1,0:T(8,128)(2,1)}) %all-gather.11.cloned.1.call-update) | async-done | bytes 1048592 | tf_op jit(solution)/shard_map/all_gather | solution.py:61
  340.4 1.7 fusion.8
  342.1 0.0 copy-start.7
  342.1 0.3 multiply_reduce_fusion.1
  342.4 0.0 copy-done.8
  342.4 0.0 copy-done.5
  342.4 1.6 fusion.2
  344.0 0.0 copy-start.4
  344.0 0.0 copy-start
  344.1 0.0 copy-start.9
  344.1 298.7 %all-gather.7.cloned.1.call-done = bf16[1024,1024]{1,0:T(8,128)(2,1)} async-done(((bf16[16,1024]{1,0:T(8,128)(2,1)}), bf16[1024,1024]{1,0:T(8,128)(2,1)}) %all-gather.7.cloned.1.call-update) | async-done | bytes 2097168 | tf_op jit(solution)/shard_map/all_gather | solution.py:60
  642.8 2.5 multiply_reduce_fusion
  645.4 156.0 %all-reduce = (f32[1024]{0:T(1024)S(1)}, f32[512]{0:T(512)S(1)}) all-reduce(f32[1024]{0:T(1024)S(1)} %get-tuple-element.12, f32[512]{0:T(512)S(1)} %get-tuple-element.14), channel_id=1, replica_groups=mesh['grp'=8,'shard'=64] {'shard'}, use_global_device_ids=true, to_apply=%region_2.0 | all-reduce | flops 1536 | bytes 12288 | tf_op jit(solution)/shard_map/psum | solution.py:91
  801.3 0.6 divide_convert_fusion
  802.0 0.0 all-gather.15.cloned.1.call-update
  802.0 0.0 all-gather.13.cloned.1.call-start
  802.0 0.0 copy-start.2
  802.1 140.5 %all-gather.9.cloned.1.call-done = bf16[1024,512]{1,0:T(8,128)(2,1)} async-done(((bf16[16,512]{1,0:T(8,128)(2,1)}), bf16[1024,512]{1,0:T(8,128)(2,1)}) %all-gather.9.cloned.1.call-update) | async-done | bytes 1048592 | tf_op jit(solution)/shard_map/all_gather | solution.py:71
  942.6 1.7 convolution_convert_fusion.3
  944.3 0.0 copy-done.7
  944.3 0.0 copy-done
  944.3 0.0 copy-done.9
  944.3 1.5 fusion.18
  945.8 0.0 copy-done.4
  945.8 0.0 copy-start.6
  945.8 1.0 convolution_convert_fusion.4
  946.8 0.0 all-gather.13.cloned.1.call-update
  946.8 0.0 all-gather.17.cloned.1.call-start
  946.8 298.1 %all-gather.15.cloned.1.call-done = bf16[1024,1024]{1,0:T(8,128)(2,1)} async-done(((bf16[16,1024]{1,0:T(8,128)(2,1)}), bf16[1024,1024]{1,0:T(8,128)(2,1)}) %all-gather.15.cloned.1.call-update) | async-done | bytes 2097168 | tf_op jit(solution)/shard_map/all_gather | solution.py:35
  1244.9 0.0 copy-done.2
  1244.9 3.8 fusion.3
  1248.7 0.0 copy-done.6
  1248.7 0.0 copy-start.3
  1248.7 0.0 copy-start.10
  1248.7 0.0 all-gather.17.cloned.1.call-update
  1248.8 0.0 copy-start.1
  1248.8 154.3 %all_gather.34 = bf16[512,512]{1,0:T(8,128)(2,1)S(1)} all-gather(bf16[8,512]{1,0:T(8,128)(2,1)S(1)} %divide_convert_fusion.1), channel_id=1, replica_groups=mesh['grp'=8,'shard'=64] {'shard'}, dimensions={0}, use_global_device_ids=true | all-gather | bytes 532480 | tf_op jit(solution)/shard_map/all_gather | solution.py:42
  1403.1 0.4 fusion.11
  1403.5 157.4 %all_gather.35 = bf16[512,512]{1,0:T(8,128)(2,1)S(1)} all-gather(bf16[8,512]{1,0:T(8,128)(2,1)S(1)} %fusion.11), channel_id=1, replica_groups=mesh['grp'=8,'shard'=64] {'shard'}, dimensions={0}, use_global_device_ids=true | all-gather | bytes 532480 | tf_op jit(solution)/shard_map/all_gather | solution.py:42
  1560.9 1.0 fusion.9
  1561.9 0.0 all-gather.13.cloned.1.call-done
  1561.9 0.0 copy-done.3
  1561.9 0.0 copy-done.10
  1561.9 2.1 fusion.5
  1564.0 282.3 %all-gather.17.cloned.1.call-done = bf16[1024,1024]{1,0:T(8,128)(2,1)} async-done(((bf16[16,1024]{1,0:T(8,128)(2,1)}), bf16[1024,1024]{1,0:T(8,128)(2,1)}) %all-gather.17.cloned.1.call-update) | async-done | bytes 2097168 | tf_op jit(solution)/shard_map/all_gather | solution.py:35
  1846.3 0.0 copy-done.1
  1846.3 3.8 fusion
  (3 shorter events, 0.0 us)
Async XLA Ops:
  7.2 335.3 %copy-start.8 = (f32[16,1024]{1,0:T(8,128)S(1)}, f32[16,1024]{1,0:T(8,128)}, u32[]{:S(2)}) copy-start(f32[16,1024]{1,0:T(8,128)} %param.12) | copy-start | bytes 196612
  7.2 333.2 %all-gather.11.cloned.1.call-start = ((), (), s32[]{:S(2)}) async-start(), calls=%async_computation.2 | async-start | bytes 1064960 | tf_op jit(solution)/shard_map/all_gather | solution.py:61
  44.8 297.6 %copy-start.5 = (bf16[16,512]{1,0:T(8,128)(2,1)S(1)}, bf16[16,512]{1,0:T(8,128)(2,1)}, u32[]{:S(2)}) copy-start(bf16[16,512]{1,0:T(8,128)(2,1)} %get-tuple-element.11) | copy-start | bytes 49156
  44.8 598.0 %all-gather.7.cloned.1.call-start = ((), (), s32[]{:S(2)}) async-start(), calls=%async_computation | async-start | bytes 2129920 | tf_op jit(solution)/shard_map/all_gather | solution.py:60
  46.4 896.2 %all-gather.9.cloned.1.call-start = ((), (), s32[]{:S(2)}) async-start(), calls=%async_computation.1 | async-start | bytes 1064960 | tf_op jit(solution)/shard_map/all_gather | solution.py:71
  47.1 1197.8 %all-gather.15.cloned.1.call-start = ((), (), s32[]{:S(2)}) async-start(), calls=%async_computation.4 | async-start | bytes 2129920 | tf_op jit(solution)/shard_map/all_gather | solution.py:35
  342.1 602.2 %copy-start.7 = (f32[8,512]{1,0:T(8,128)}, f32[8,512]{1,0:T(8,128)S(1)}, u32[]{:S(2)}) copy-start(f32[8,512]{1,0:T(8,128)S(1)} %fusion.8) | copy-start | bytes 49156
  344.0 601.7 %copy-start.4 = (f32[16,1024]{1,0:T(8,128)}, f32[16,1024]{1,0:T(8,128)S(1)}, u32[]{:S(2)}) copy-start(f32[16,1024]{1,0:T(8,128)S(1)} %fusion.2) | copy-start | bytes 196612
  344.0 600.2 %copy-start = (bf16[1024,512]{1,0:T(8,128)(2,1)S(1)}, bf16[1024,512]{1,0:T(8,128)(2,1)}, u32[]{:S(2)}) copy-start(bf16[1024,512]{1,0:T(8,128)(2,1)} %all-gather.11.cloned.1.call-done) | copy-start | bytes 3145732
  344.1 600.2 %copy-start.9 = (f32[16,512]{1,0:T(8,128)S(1)}, f32[16,512]{1,0:T(8,128)}, u32[]{:S(2)}) copy-start(f32[16,512]{1,0:T(8,128)} %param.11) | copy-start | bytes 98308
  802.0 759.9 %all-gather.13.cloned.1.call-start = ((), (), s32[]{:S(2)}) async-start(), calls=%async_computation.3 | async-start | bytes 1064960 | tf_op jit(solution)/shard_map/all_gather | solution.py:86
  802.0 442.9 %copy-start.2 = (bf16[16,1024]{1,0:T(8,128)(2,1)S(1)}, bf16[16,1024]{1,0:T(8,128)(2,1)}, u32[]{:S(2)}) copy-start(bf16[16,1024]{1,0:T(8,128)(2,1)} %divide_convert_fusion) | copy-start | bytes 98308
  945.8 303.0 %copy-start.6 = (f32[16,512]{1,0:T(8,128)}, f32[16,512]{1,0:T(8,128)S(1)}, u32[]{:S(2)}) copy-start(f32[16,512]{1,0:T(8,128)S(1)} %fusion.18) | copy-start | bytes 98308
  946.8 899.6 %all-gather.17.cloned.1.call-start = ((), (), s32[]{:S(2)}) async-start(), calls=%async_computation.5 | async-start | bytes 2129920 | tf_op jit(solution)/shard_map/all_gather | solution.py:35
  1248.7 313.2 %copy-start.3 = (bf16[16,1024]{1,0:T(8,128)(2,1)S(1)}, bf16[16,1024]{1,0:T(8,128)(2,1)}, u32[]{:S(2)}) copy-start(bf16[16,1024]{1,0:T(8,128)(2,1)} %convert_element_type.62) | copy-start | bytes 98308
  1248.7 313.2 %copy-start.10 = (f32[16,512]{1,0:T(8,128)S(1)}, f32[16,512]{1,0:T(8,128)}, u32[]{:S(2)}) copy-start(f32[16,512]{1,0:T(8,128)} %param.9) | copy-start | bytes 98308
  1248.8 597.6 %copy-start.1 = (bf16[16,1024]{1,0:T(8,128)(2,1)S(1)}, bf16[16,1024]{1,0:T(8,128)(2,1)}, u32[]{:S(2)}) copy-start(bf16[16,1024]{1,0:T(8,128)(2,1)} %fusion.3) | copy-start | bytes 98308
Sparse Core Ops, SparseCore 0:
  44.9 295.3 all-gather.10
  343.0 299.7 all-gather.6
  645.5 297.0 all-gather.8
  945.1 299.8 all-gather.14
  1246.9 297.0 all-gather.12
  1546.5 299.7 all-gather.16
where the time goes:
time: 1860 us
  waiting for transfers between devices  1160 us (62%)
  blocking collectives  658 us (35%)
  matrix products  21.4 us (1%)
    all_gather x2, waiting for transfers between devices, left_sweep(): segment = lax.all_gather(current, 'shard', axis=0, tiled=True)  580 us
    all_gather x2, blocking collectives, right_sweep(): segment = lax.all_gather(current, 'shard', axis=0, tiled=True)  312 us
    all_gather x1, waiting for transfers between devices, local(): basis_part = lax.all_gather(left_half, 'shard', axis=0, tiled=True)  299 us
    psum x1, blocking collectives, local(): lax.psum((jnp.sum(left_power * left_power, axis=0), jnp.sum(right_power *...  156 us
    all_gather x1, blocking collectives, local(): lax.all_gather(right_basis.astype(jnp.bfloat16), 'shard', axis=0, tiled=T...  154 us
    all_gather x1, waiting for transfers between devices, local(): lax.all_gather(moment_half, 'shard', axis=0, tiled=True)  141 us
    all_gather x1, waiting for transfers between devices, local(): grad_part = lax.all_gather(grad_half, 'shard', axis=0, tiled=True)  138 us
  transfers between devices with their start and end apart: 6, of which 5 were waited for; matrix products, arithmetic and copies ran while one was open for 1% of the time, Pallas kernels for 0%

commit v1 on v0

--- a/solution.py
+++ b/solution.py
@@ -57,7 +57,8 @@
     left_half = left_basis.astype(jnp.bfloat16)
     right_whole = lax.all_gather(right_basis.astype(jnp.bfloat16), "shard", axis=0, tiled=True)
     right_wide = lax.optimization_barrier(right_whole).astype(jnp.float32)
-    basis_part = lax.all_gather(left_half, "shard", axis=0, tiled=True)
+    sent = jnp.stack([left_half] * lax.axis_size("shard"))
+    basis_part = jnp.concatenate(lax.all_to_all(sent, "shard", 0, 0), axis=0)
     grad_part = lax.all_gather(grad_half, "shard", axis=0, tiled=True)
     basis_columns = lax.dynamic_slice_in_dim(basis_part, row_first, local_rows, 1)
     turned = inner_rows(basis_columns, grad_part)

time: 1860 us -> 1570 us (0.84)
  waiting for transfers between devices: 1160 us -> 859 us
    all_gather x1 -> x0, waiting for transfers between devices: 299 us -> none  [local(): basis_part = lax.all_gather(left_half, 'shard', axis=0, tiled=True)]
  transfers between devices with their start and end apart: 6 -> 6, of which waited for: 5 -> 4; matrix products, arithmetic and copies ran while one was open for 1% -> 1% of each run, Pallas kernels for 0% -> 0%
where the time goes in v1:
time: 1570 us
  waiting for transfers between devices  859 us (55%)
  blocking collectives  662 us (42%)
  matrix products  20 us (1%)
    all_gather x2, waiting for transfers between devices, left_sweep(): segment = lax.all_gather(current, 'shard', axis=0, tiled=True)  580 us
    all_gather x2, blocking collectives, right_sweep(): segment = lax.all_gather(current, 'shard', axis=0, tiled=True)  312 us
    all_gather x1, blocking collectives, local(): lax.all_gather(right_basis.astype(jnp.bfloat16), 'shard', axis=0, tiled=T...  159 us
    psum x1, blocking collectives, local(): lax.psum((jnp.sum(left_power * left_power, axis=0), jnp.sum(right_power *...  156 us
    all_gather x1, waiting for transfers between devices, local(): grad_part = lax.all_gather(grad_half, 'shard', axis=0, tiled=True)  140 us
    all_gather x1, waiting for transfers between devices, local(): lax.all_gather(moment_half, 'shard', axis=0, tiled=True)  138 us
    psum x1, blocking collectives, local(): gradient = lax.psum(gradients[0], 'grp') / lax.axis_size('grp')  35.3 us
  transfers between devices with their start and end apart: 6, of which 4 were waited for; matrix products, arithmetic and copies ran while one was open for 1% of the time, Pallas kernels for 0%

profile of v1, /device:TPU:2, one launch (start us, length us, event | category | flops | bytes accessed | tf_op | source)
XLA Modules:
  0.0 1571.8 jit_solution(4135359234645867324)
XLA Ops:
  7.2 0.8 convert_element_type.62
  8.0 1.6 stack.2
  9.6 0.0 copy-start.9
  9.6 0.0 copy-start.10
  9.6 0.0 copy-start.12
  9.6 0.0 copy-start.11
  9.6 12.6 all-to-all-start
  22.2 0.0 copy-start.6
  22.2 0.0 all-gather.8.cloned.1.call-start
  22.3 0.0 copy-done.9
  22.3 35.3 %psum.21 = f32[16,512]{1,0:T(8,128)S(1)} all-reduce(f32[16,512]{1,0:T(8,128)S(1)} %bitcast.36), channel_id=1, replica_groups=mesh['grp'=8,'shard'=64] {'grp'}, use_global_device_ids=true, to_apply=%region_0.0 | all-reduce | flops 8192 | bytes 65536 | tf_op jit(solution)/shard_map/psum | solution.py:53
  57.6 0.0 copy-done.10
  57.6 0.6 fusion.29
  58.3 0.0 copy-start.3
  58.3 0.0 all-gather.8.cloned.1.call-update
  58.3 0.0 all-gather.6.cloned.1.call-start
  58.3 0.7 all-gather.6.cloned.1.call-update
  59.0 0.0 all-gather.12.cloned.1.call-start
  59.1 0.0 copy-done.12
  59.1 159.1 %all_gather.25 = bf16[512,512]{1,0:T(8,128)(2,1)S(1)} all-gather(bf16[8,512]{1,0:T(8,128)(2,1)S(1)} %convert_element_type.65), channel_id=1, replica_groups=mesh['grp'=8,'shard'=64] {'shard'}, dimensions={0}, use_global_device_ids=true | all-gather | bytes 532480 | tf_op jit(solution)/shard_map/all_gather | solution.py:58
  218.2 139.8 %all-gather.8.cloned.1.call-done = bf16[1024,512]{1,0:T(8,128)(2,1)} async-done(((bf16[16,512]{1,0:T(8,128)(2,1)}), bf16[1024,512]{1,0:T(8,128)(2,1)}) %all-gather.8.cloned.1.call-update) | async-done | bytes 1048592 | tf_op jit(solution)/shard_map/all_gather | solution.py:62
  358.0 0.0 copy-done.11
  358.0 1.7 fusion.8
  359.7 0.0 copy-start.5
  359.7 0.3 multiply_reduce_fusion.1
  360.1 0.0 copy-done.6
  360.1 0.0 copy-done.3
  360.1 1.6 fusion.2
  361.7 0.0 copy-start.2
  361.7 0.0 copy-start.7
  361.7 0.0 all-to-all-done
  361.7 0.9 multiply_reduce_fusion
  362.7 155.8 %all-reduce = (f32[1024]{0:T(1024)S(1)}, f32[512]{0:T(512)S(1)}) all-reduce(f32[1024]{0:T(1024)S(1)} %get-tuple-element.12, f32[512]{0:T(512)S(1)} %get-tuple-element.14), channel_id=1, replica_groups=mesh['grp'=8,'shard'=64] {'shard'}, use_global_device_ids=true, to_apply=%region_2.0 | all-reduce | flops 1536 | bytes 12288 | tf_op jit(solution)/shard_map/psum | solution.py:92
  518.5 0.6 divide_convert_fusion
  519.1 0.0 all-gather.12.cloned.1.call-update
  519.1 0.0 all-gather.10.cloned.1.call-start
  519.2 0.0 copy-start.1
  519.2 138.4 %all-gather.6.cloned.1.call-done = bf16[1024,512]{1,0:T(8,128)(2,1)} async-done(((bf16[16,512]{1,0:T(8,128)(2,1)}), bf16[1024,512]{1,0:T(8,128)(2,1)}) %all-gather.6.cloned.1.call-update) | async-done | bytes 1048592 | tf_op jit(solution)/shard_map/all_gather | solution.py:72
  657.6 1.6 convolution_convert_fusion.3
  659.2 0.0 copy-done.5
  659.2 0.0 copy-done.7
  659.2 1.8 fusion.18
  660.9 0.0 copy-done.2
  661.0 0.0 copy-start.4
  661.0 1.0 convolution_convert_fusion.4
  661.9 0.0 all-gather.10.cloned.1.call-update
  662.0 0.0 all-gather.14.cloned.1.call-start
  662.0 298.1 %all-gather.12.cloned.1.call-done = bf16[1024,1024]{1,0:T(8,128)(2,1)} async-done(((bf16[16,1024]{1,0:T(8,128)(2,1)}), bf16[1024,1024]{1,0:T(8,128)(2,1)}) %all-gather.12.cloned.1.call-update) | async-done | bytes 2097168 | tf_op jit(solution)/shard_map/all_gather | solution.py:35
  960.1 0.0 copy-done.1
  960.1 3.8 fusion.3
  963.9 0.0 copy-done.4
  963.9 0.0 copy-start.8
  963.9 0.0 all-gather.14.cloned.1.call-update
  963.9 0.0 copy-start
  964.0 154.4 %all_gather.30 = bf16[512,512]{1,0:T(8,128)(2,1)S(1)} all-gather(bf16[8,512]{1,0:T(8,128)(2,1)S(1)} %divide_convert_fusion.1), channel_id=1, replica_groups=mesh['grp'=8,'shard'=64] {'shard'}, dimensions={0}, use_global_device_ids=true | all-gather | bytes 532480 | tf_op jit(solution)/shard_map/all_gather | solution.py:42
  1118.3 0.4 fusion.11
  1118.7 157.3 %all_gather.31 = bf16[512,512]{1,0:T(8,128)(2,1)S(1)} all-gather(bf16[8,512]{1,0:T(8,128)(2,1)S(1)} %fusion.11), channel_id=1, replica_groups=mesh['grp'=8,'shard'=64] {'shard'}, dimensions={0}, use_global_device_ids=true | all-gather | bytes 532480 | tf_op jit(solution)/shard_map/all_gather | solution.py:42
  1276.0 1.0 fusion.9
  1277.0 0.0 all-gather.10.cloned.1.call-done
  1277.0 0.0 copy-done.8
  1277.0 2.1 fusion.5
  1279.1 282.4 %all-gather.14.cloned.1.call-done = bf16[1024,1024]{1,0:T(8,128)(2,1)} async-done(((bf16[16,1024]{1,0:T(8,128)(2,1)}), bf16[1024,1024]{1,0:T(8,128)(2,1)}) %all-gather.14.cloned.1.call-update) | async-done | bytes 2097168 | tf_op jit(solution)/shard_map/all_gather | solution.py:35
  1561.5 0.0 copy-done
  1561.5 3.8 fusion
  (4 shorter events, 0.0 us)
Async XLA Ops:
  9.6 12.7 copy-start.9
  9.6 48.0 %copy-start.10 = (f32[16,512]{1,0:T(8,128)S(1)}, f32[16,512]{1,0:T(8,128)}, u32[]{:S(2)}) copy-start(f32[16,512]{1,0:T(8,128)} %param.10) | copy-start | bytes 98308
  9.6 49.5 %copy-start.12 = (f32[8,512]{1,0:T(8,128)S(1)}, f32[8,512]{1,0:T(8,128)}, u32[]{:S(2)}) copy-start(f32[8,512]{1,0:T(8,128)} %param.15) | copy-start | bytes 49156
  9.6 348.4 %copy-start.11 = (f32[8,512]{1,0:T(8,128)S(1)}, f32[8,512]{1,0:T(8,128)}, u32[]{:S(2)}) copy-start(f32[8,512]{1,0:T(8,128)} %param.14) | copy-start | bytes 49156
  9.6 352.1 %all-to-all-start = ((bf16[64,16,1024]{2,1,0:T(8,128)(2,1)}), bf16[64,16,1024]{2,1,0:T(8,128)(2,1)S(1)}, u32[]{:S(2)}, u32[]{:S(2)}) async-start(bf16[64,16,1024]{2,1,0:T(8,128)(2,1)} %stack.2), calls=%async_computation | async-start | bytes 4194304 | tf_op jit(solution)/shard_map/all_to_all | solution.py:61
  22.2 337.8 %copy-start.6 = (f32[16,1024]{1,0:T(8,128)S(1)}, f32[16,1024]{1,0:T(8,128)}, u32[]{:S(2)}) copy-start(f32[16,1024]{1,0:T(8,128)} %param.12) | copy-start | bytes 196612
  22.2 335.7 %all-gather.8.cloned.1.call-start = ((), (), s32[]{:S(2)}) async-start(), calls=%async_computation.2 | async-start | bytes 1064960 | tf_op jit(solution)/shard_map/all_gather | solution.py:62
  58.3 301.8 %copy-start.3 = (bf16[16,512]{1,0:T(8,128)(2,1)S(1)}, bf16[16,512]{1,0:T(8,128)(2,1)}, u32[]{:S(2)}) copy-start(bf16[16,512]{1,0:T(8,128)(2,1)} %get-tuple-element.11) | copy-start | bytes 49156
  58.3 599.3 %all-gather.6.cloned.1.call-start = ((), (), s32[]{:S(2)}) async-start(), calls=%async_computation.1 | async-start | bytes 1064960 | tf_op jit(solution)/shard_map/all_gather | solution.py:72
  59.0 901.1 %all-gather.12.cloned.1.call-start = ((), (), s32[]{:S(2)}) async-start(), calls=%async_computation.4 | async-start | bytes 2129920 | tf_op jit(solution)/shard_map/all_gather | solution.py:35
  359.7 299.5 %copy-start.5 = (f32[8,512]{1,0:T(8,128)}, f32[8,512]{1,0:T(8,128)S(1)}, u32[]{:S(2)}) copy-start(f32[8,512]{1,0:T(8,128)S(1)} %fusion.8) | copy-start | bytes 49156
  361.7 299.3 %copy-start.2 = (f32[16,1024]{1,0:T(8,128)}, f32[16,1024]{1,0:T(8,128)S(1)}, u32[]{:S(2)}) copy-start(f32[16,1024]{1,0:T(8,128)S(1)} %fusion.2) | copy-start | bytes 196612
  361.7 297.5 %copy-start.7 = (f32[16,512]{1,0:T(8,128)S(1)}, f32[16,512]{1,0:T(8,128)}, u32[]{:S(2)}) copy-start(f32[16,512]{1,0:T(8,128)} %param.11) | copy-start | bytes 98308
  519.1 757.9 %all-gather.10.cloned.1.call-start = ((), (), s32[]{:S(2)}) async-start(), calls=%async_computation.3 | async-start | bytes 1064960 | tf_op jit(solution)/shard_map/all_gather | solution.py:87
  519.2 440.9 %copy-start.1 = (bf16[16,1024]{1,0:T(8,128)(2,1)S(1)}, bf16[16,1024]{1,0:T(8,128)(2,1)}, u32[]{:S(2)}) copy-start(bf16[16,1024]{1,0:T(8,128)(2,1)} %divide_convert_fusion) | copy-start | bytes 98308
  661.0 302.9 %copy-start.4 = (f32[16,512]{1,0:T(8,128)}, f32[16,512]{1,0:T(8,128)S(1)}, u32[]{:S(2)}) copy-start(f32[16,512]{1,0:T(8,128)S(1)} %fusion.18) | copy-start | bytes 98308
  662.0 899.5 %all-gather.14.cloned.1.call-start = ((), (), s32[]{:S(2)}) async-start(), calls=%async_computation.5 | async-start | bytes 2129920 | tf_op jit(solution)/shard_map/all_gather | solution.py:35
  963.9 313.1 %copy-start.8 = (f32[16,512]{1,0:T(8,128)S(1)}, f32[16,512]{1,0:T(8,128)}, u32[]{:S(2)}) copy-start(f32[16,512]{1,0:T(8,128)} %param.9) | copy-start | bytes 98308
  963.9 597.5 %copy-start = (bf16[16,1024]{1,0:T(8,128)(2,1)S(1)}, bf16[16,1024]{1,0:T(8,128)(2,1)}, u32[]{:S(2)}) copy-start(bf16[16,1024]{1,0:T(8,128)(2,1)} %fusion.3) | copy-start | bytes 98308
Sparse Core Ops, SparseCore 0:
  58.4 299.5 all-gather.7
  360.6 296.9 all-gather.5
  660.2 299.8 all-gather.11
  962.0 297.1 all-gather.9
  1261.7 299.7 all-gather.13
